TPU v7x, 256 devices: a whole 4x4x8 slice. The times are simulated.
256 devices in a mesh: sp: 64 (over z, y, x_hi), hd: 4 (over x_lo, core).
Axes of the slice: x: 4 (x_hi: 2, x_lo: 2; x = x_hi * 2 + x_lo), y: 4, z: 8, core: 2. Of those that a mesh axis runs over, the one named last changes fastest.
Arguments:
- features: bfloat16 [524288, 256], P(('sp', 'hd')), may hold values from -48 to 48
- point_dest: int32 [524288], P(('sp', 'hd')), may hold values from 0 to 524287, as said below
- cluster: int32 [524288], P(('sp', 'hd')), may hold values from 0 to 131071, as said below
- owner_row: int32 [131072], P(('sp', 'hd')), may hold values from 0 to 131071, as said below
- w_qkv: bfloat16 [3, 256, 256], replicated, may hold values from -1 to 1
- w_out: bfloat16 [256, 256], replicated, may hold values from -0.375 to 0.375
- w_up: bfloat16 [256, 1024], replicated, may hold values from -0.375 to 0.375
- w_down: bfloat16 [1024, 256], replicated, may hold values from -0.1875 to 0.1875
- w_pool: bfloat16 [256, 512], replicated, may hold values from -0.375 to 0.375
Outputs:
- pooled: bfloat16 [131072, 512], P(('sp', 'hd'))
Inputs may be any that keep to these rules, and one draw needn't show every extreme that they name: `point_dest`: a permutation; at most 12 of the points of one device (a block of 2048 consecutive entries) go to any one block of 2048 consecutive positions of the new order. `cluster`: on device s (entries s * 2048 to (s + 1) * 2048 - 1) the ids never fall along the points, and each id from s * 512 to (s + 1) * 512 - 1 names one or more of its points. `owner_row`: a permutation; at most 4 of the voxels of one device (a block of 512 consecutive entries) go to any one block of 512 consecutive output rows.
All inputs are finite; a program needn't handle non-finite values.
Results may differ from a plain program's by a relative error of at most 0.0071.
Values may be sent and summed in bfloat16 or wider, within the bound.
A program may use at most 64 MiB of HBM per device.

v0:
```python
import functools
import jax
import jax.numpy as jnp
from jax import lax
from jax.experimental import pallas as pl
from jax.experimental.pallas import tpu as pltpu
from jax.sharding import PartitionSpec as P

BF = jnp.bfloat16
F32 = jnp.float32
I32 = jnp.int32
HS = 16
PATCH = 1024
EPSILON = 1e-05
LOG2E = 1.4426950408889634
SCALE = HS ** (-0.5) * LOG2E
SAFE = 100.0


def normalize(values):
    center = jnp.mean(values, axis=-1, keepdims=True)
    shifted = values - center
    spread = jnp.mean(shifted * shifted, axis=-1, keepdims=True)
    return shifted * lax.rsqrt(spread + EPSILON)


def gelu(values):
    return 0.5 * values * (1.0 + lax.erf(values * (0.5**0.5)))


def mm(a, b):
    return jnp.dot(a, b, preferred_element_type=F32)


def layer_kernel(
    points_ref, ids_ref, wqkv_ref, wout_ref, wup_ref, wdown_ref, means_ref,
    wq_s, wv_s, k_s, q_s, v_s, att_s, fin_s,
):
    rows_all, width = points_ref.shape
    heads = width // HS
    blk = 256
    groups = width // 128
    wq_s[...] = wqkv_ref[0].T
    wv_s[...] = wqkv_ref[2].T
    v_s[:, HS:, :] = jnp.ones((heads, HS, PATCH), BF)
    head_mask = (
        lax.broadcasted_iota(I32, (width, 128), 0) // HS
        == lax.broadcasted_iota(I32, (width, 128), 1)
    ).astype(BF)

    def patch(number, carry):
        base = number * PATCH

        def project(i, bound):
            qmax, kmax = bound
            r0 = pl.multiple_of(i * blk, blk)
            x = points_ref[pl.ds(pl.multiple_of(base + r0, blk), blk), :].astype(F32)
            normed = normalize(x).astype(BF)
            keys = mm(normed, wqkv_ref[1])
            for g in range(groups):
                k_s[g, pl.ds(r0, blk), :] = keys[:, g * 128 : (g + 1) * 128].astype(BF)
            nt = (((1,), (1,)), ((), ()))
            queries = lax.dot_general(wq_s[...], normed, nt, preferred_element_type=F32)
            values = lax.dot_general(wv_s[...], normed, nt, preferred_element_type=F32)
            q_s[:, pl.ds(r0, blk)] = queries.astype(BF)
            v_s[:, 0:HS, pl.ds(r0, blk)] = values.astype(BF).reshape(heads, HS, blk)
            knorm = mm((keys * keys).astype(BF), head_mask)
            qnorm = jnp.sum((queries * queries).reshape(heads, HS, blk), axis=1)
            return (jnp.maximum(qmax, qnorm), jnp.maximum(kmax, jnp.max(knorm, axis=0, keepdims=True)))

        qmax, kmax = lax.fori_loop(
            0, PATCH // blk, project,
            (jnp.zeros((heads, blk), F32), jnp.zeros((1, 128), F32)),
        )
        bound = 1.05 * SCALE * SCALE * jnp.max(qmax) * jnp.max(kmax)
        qb = 512
        sub = lax.broadcasted_iota(I32, (128, qb), 0) // HS

        def attend(shifted):
            def head(h, c):
                g = h // 8
                r0 = pl.multiple_of(h * HS, HS)
                for q0 in range(0, PATCH, qb):
                    q = q_s[pl.ds(r0, HS), q0 : q0 + qb]
                    q = jnp.concatenate([q] * 8, axis=0)
                    q = jnp.where(sub == h % 8, q, jnp.zeros_like(q))
                    scores = mm(k_s[g], q)
                    if shifted:
                        scores = scores - jnp.max(scores, axis=0, keepdims=True)
                    raised = jnp.exp2(scores * SCALE).astype(BF)
                    out = mm(v_s[h], raised)
                    att_s[pl.ds(r0, HS), q0 : q0 + qb] = (out[:HS] / out[HS : HS + 1]).astype(BF)
                return c

            lax.fori_loop(0, heads, head, 0)

        @pl.when(bound <= SAFE * SAFE)
        def _():
            attend(False)

        @pl.when(jnp.logical_not(bound <= SAFE * SAFE))
        def _():
            attend(True)

        def mlp(i, c):
            r0 = pl.multiple_of(i * blk, blk)
            rows = pl.ds(pl.multiple_of(base + r0, blk), blk)
            attended = att_s[:, pl.ds(r0, blk)].T
            middle = points_ref[rows, :].astype(F32) + mm(attended, wout_ref[...])
            normed = normalize(middle).astype(BF)
            total = middle
            hidden = gelu(mm(normed, wup_ref[...])).astype(BF)
            total = total + mm(hidden, wdown_ref[...])
            fin_s[rows, :] = total.astype(BF)
            return c

        lax.fori_loop(0, PATCH // blk, mlp, 0)
        return carry

    lax.fori_loop(0, rows_all // PATCH, patch, 0)

    voxels = means_ref.shape[0]
    vb = 128

    def pool(i, c):
        v0 = pl.multiple_of(i * vb, vb)
        marks = (
            lax.broadcasted_iota(I32, (vb, rows_all), 0) + v0 == ids_ref[...]
        )
        marks = jnp.where(marks, 1.0, 0.0).astype(F32)
        tally = jnp.sum(marks, axis=1, keepdims=True)
        totals = mm(marks.astype(BF), fin_s[...])
        means_ref[pl.ds(v0, vb), :] = (totals / tally).astype(BF)
        return c

    lax.fori_loop(0, voxels // vb, pool, 0)


def layer(points, ids, w_qkv, w_out, w_up, w_down, voxels):
    rows, width = points.shape
    heads = width // HS
    vm = pl.BlockSpec(memory_space=pltpu.VMEM)
    return pl.pallas_call(
        layer_kernel,
        out_shape=jax.ShapeDtypeStruct((voxels, width), BF),
        in_specs=[vm] * 6,
        out_specs=vm,
        scratch_shapes=[
            pltpu.VMEM((width, width), BF),
            pltpu.VMEM((width, width), BF),
            pltpu.VMEM((width // 128, PATCH, 128), BF),
            pltpu.VMEM((width, PATCH), BF),
            pltpu.VMEM((heads, 2 * HS, PATCH), BF),
            pltpu.VMEM((width, PATCH), BF),
            pltpu.VMEM((rows, width), BF),
        ],
        compiler_params=pltpu.CompilerParams(vmem_limit_bytes=56 * 2**20),
        name="layer",
    )(points, ids, w_qkv, w_out, w_up, w_down)


def pack_rows(row_data, target, block_len, peer_count, capacity):
    owner_block = target // block_len
    slot_number = target % block_len
    onehot = (owner_block[:, None] == jnp.arange(peer_count, dtype=jnp.int32)[None, :]).astype(
        jnp.int32
    )
    before = jnp.cumsum(onehot, axis=0) - onehot
    positions = owner_block * capacity + jnp.sum(before * onehot, axis=1)
    packed = (
        jnp.zeros((peer_count * capacity, row_data.shape[1]), row_data.dtype)
        .at[positions]
        .set(row_data)
    )
    slot_ids = (
        jnp.full((peer_count * capacity,), block_len, jnp.int32).at[positions].set(slot_number)
    )
    return (packed, slot_ids)


def place_rows(arrived, slot_ids, block_len):
    return (
        jnp.zeros((block_len, arrived.shape[1]), arrived.dtype)
        .at[slot_ids]
        .set(arrived, mode="drop")
    )


def pack_voxels(row_data, owner_row, voxel_local, outer_count, inner_count):
    device_count = outer_count * inner_count
    capacity = 2 * (voxel_local // device_count)
    width = row_data.shape[1]
    packed, slot_ids = pack_rows(row_data, owner_row, voxel_local, device_count, capacity)
    return (
        packed.reshape(outer_count, inner_count, capacity, width),
        slot_ids.reshape(outer_count, inner_count, capacity),
    )


def per_device(features, point_dest, cluster, owner_row, w_qkv, w_out, w_up, w_down, w_pool):
    local_points = features.shape[0]
    model_width = features.shape[1]
    voxel_local = owner_row.shape[0]
    outer_count = lax.axis_size("sp")
    inner_count = lax.axis_size("hd")
    device_count = outer_count * inner_count
    device_number = lax.axis_index("sp") * inner_count + lax.axis_index("hd")
    base_rows = local_points // device_count
    capacity = base_rows + base_rows // 2
    packed, slot_ids = pack_rows(features, point_dest, local_points, device_count, capacity)
    packed = packed.reshape(outer_count, inner_count, capacity, model_width)
    slot_ids = slot_ids.reshape(outer_count, inner_count, capacity)
    arrived, arrived_slots = (
        lax.all_to_all(
            lax.all_to_all(packed, "sp", split_axis=0, concat_axis=0, tiled=True),
            "hd",
            split_axis=1,
            concat_axis=1,
            tiled=True,
        ),
        lax.all_to_all(
            lax.all_to_all(slot_ids, "sp", split_axis=0, concat_axis=0, tiled=True),
            "hd",
            split_axis=1,
            concat_axis=1,
            tiled=True,
        ),
    )
    points = place_rows(arrived.reshape(-1, model_width), arrived_slots.reshape(-1), local_points)
    local_ids = cluster - device_number * voxel_local
    means = layer(
        points, local_ids.reshape(1, local_points), w_qkv, w_out, w_up, w_down, voxel_local
    )
    sent_rows, sent_slots = pack_voxels(means, owner_row, voxel_local, outer_count, inner_count)
    got_rows, got_slots = (
        lax.all_to_all(
            lax.all_to_all(sent_rows, "sp", split_axis=0, concat_axis=0, tiled=True),
            "hd",
            split_axis=1,
            concat_axis=1,
            tiled=True,
        ),
        lax.all_to_all(
            lax.all_to_all(sent_slots, "sp", split_axis=0, concat_axis=0, tiled=True),
            "hd",
            split_axis=1,
            concat_axis=1,
            tiled=True,
        ),
    )
    placed = place_rows(
        got_rows.reshape(-1, means.shape[1]), got_slots.reshape(-1), voxel_local
    )
    projected = mm(placed, w_pool)
    return gelu(normalize(projected)).astype(BF)


def solution(mesh):
    return jax.shard_map(
        per_device,
        mesh=mesh,
        in_specs=(
            P(("sp", "hd"), None),
            P(("sp", "hd")),
            P(("sp", "hd")),
            P(("sp", "hd")),
            P(),
            P(),
            P(),
            P(),
            P(),
        ),
        out_specs=P(("sp", "hd"), None),
        check_vma=False,
    )
```

profile of v0, /device:TPU:1, one launch (start us, length us, event | category | flops | bytes accessed | tf_op | source)
XLA Modules:
  0.0 292.1 jit_solution(16081078418988195286)
XLA Ops:
  0.0 0.0 copy-start
  0.0 0.8 add_select_fusion
  0.8 0.1 copy.32
  0.9 0.3 fusion.2
  1.3 0.2 broadcast_add_fusion
  1.5 1.2 copy.33
  2.7 0.9 fusion.1
  3.7 8.1 %scatter_custom_fusion.1 = s32[3072]{0:T(1024)S(1)} fusion(s32[2048]{0:T(1024)S(1)} %compare_select_fusion.2, s32[2048]{0:T(1024)S(1)} %get-tuple-element.5, s32[]{:T(128)} %constant.91.clone.1), kind=kCustom, calls=%fused_computation.45 | custom fusion | bytes 12292 | tf_op jit(solution)/shard_map/scatter | solution.py:176
  11.8 0.8 reshape.131
  12.6 15.1 %all-to-all-start.2 = ((s32[64,4,12]{2,1,0:T(4,128)}), s32[64,4,12]{2,1,0:T(4,128)S(1)}, u32[]{:S(2)}, u32[]{:S(2)}) async-start(s32[64,4,12]{2,1,0:T(4,128)} %reshape.131), calls=%async_computation.2 | async-start | bytes 262144 | tf_op jit(solution)/shard_map/all_to_all | solution.py:222
  27.7 11.0 %scatter_custom_fusion.2 = bf16[3072,256]{1,0:T(8,128)(2,1)} fusion(s32[2048]{0:T(1024)S(1)} %compare_select_fusion.2, bf16[2048,256]{1,0:T(8,128)(2,1)} %param.9, bf16[]{:T(256)} %constant.82.clone.1), kind=kCustom, calls=%fused_computation.17 | custom fusion | bytes 1573376 | tf_op jit(solution)/shard_map/scatter | solution.py:173
  38.7 2.3 reshape.133
  41.0 2.0 copy.36
  43.0 0.0 all-to-all-done.2
  43.0 12.3 %all-to-all-start.4 = ((bf16[64,4,12,256]{3,1,2,0:T(4,128)(2,1)}), bf16[64,4,12,256]{3,1,2,0:T(4,128)(2,1)S(1)}, u32[]{:S(2)}, u32[]{:S(2)}) async-start(bf16[64,4,12,256]{3,1,2,0:T(4,128)(2,1)} %copy.36), calls=%async_computation.4 | async-start | bytes 3145728 | tf_op jit(solution)/shard_map/all_to_all | solution.py:215
  55.3 0.1 copy.34
  55.4 0.7 reshape.204
  56.1 37.4 %all-to-all-done.4 = bf16[64,4,12,256]{3,1,2,0:T(4,128)(2,1)S(1)} async-done(((bf16[64,4,12,256]{3,1,2,0:T(4,128)(2,1)}), bf16[64,4,12,256]{3,1,2,0:T(4,128)(2,1)S(1)}, u32[]{:S(2)}, u32[]{:S(2)}) %all-to-all-start.4) | async-done | bytes 1572896 | tf_op jit(solution)/shard_map/all_to_all | solution.py:215
  93.5 7.6 %all-to-all-start.3 = ((s32[4,1,768]{2,1,0:T(1,128)}), s32[4,1,768]{2,1,0:T(1,128)S(1)}, u32[]{:S(2)}, u32[]{:S(2)}) async-start(s32[4,1,768]{2,1,0:T(1,128)} %reshape.204), calls=%async_computation.3 | async-start | bytes 24576 | tf_op jit(solution)/shard_map/all_to_all | solution.py:221
  101.1 0.1 copy.28
  101.2 1.7 copy.37
  102.9 1.3 all-to-all-done.3
  104.2 4.3 %all-to-all-start.5 = ((bf16[64,4,12,256]{3,0,2,1:T(8,128)(2,1)}), bf16[64,4,12,256]{3,0,2,1:T(8,128)(2,1)S(1)}, u32[]{:S(2)}, u32[]{:S(2)}) async-start(bf16[64,4,12,256]{3,0,2,1:T(8,128)(2,1)} %copy.37), calls=%async_computation.5 | async-start | bytes 3145728 | tf_op jit(solution)/shard_map/all_to_all | solution.py:214
  108.5 0.2 fusion.11
  108.8 0.1 copy.29
  108.9 0.2 fusion.8
  109.1 2.6 scatter_custom_fusion
  111.8 0.8 reshape.128
  112.6 0.0 copy-done.2
  112.6 0.6 broadcast_subtract_fusion
  113.2 0.5 broadcast.162
  113.7 0.6 reduce.1
  114.3 0.1 reshape.205
  114.4 0.1 copy.35
  114.5 0.2 reshape.132
  114.7 12.8 %all-to-all-done.5 = bf16[64,4,12,256]{3,0,2,1:T(8,128)(2,1)S(1)} async-done(((bf16[64,4,12,256]{3,0,2,1:T(8,128)(2,1)}), bf16[64,4,12,256]{3,0,2,1:T(8,128)(2,1)S(1)}, u32[]{:S(2)}, u32[]{:S(2)}) %all-to-all-start.5) | async-done | bytes 1572896 | tf_op jit(solution)/shard_map/all_to_all | solution.py:214
  127.5 5.6 %all-to-all-start = ((s32[64,4,4]{2,1,0:T(4,128)}), s32[64,4,4]{2,1,0:T(4,128)S(1)}, u32[]{:S(2)}, u32[]{:S(2)}) async-start(s32[64,4,4]{2,1,0:T(4,128)} %reshape.128), calls=%async_computation | async-start | bytes 262144 | tf_op jit(solution)/shard_map/all_to_all | solution.py:244
  133.2 2.3 copy.38
  135.5 1.3 reshape.166
  136.9 14.9 %scatter_custom_fusion.3.points_ref = bf16[2048,256]{1,0:T(8,128)(2,1)} fusion(s32[3072]{0:T(1024)S(1)} %bitcast.44, bf16[3072,256]{1,0:T(8,128)(2,1)} %reshape.166, bf16[]{:T(256)} %constant.82.clone.1), kind=kCustom, calls=%fused_computation.22 | custom fusion | bytes 1049088 | tf_op jit(solution)/shard_map/scatter | solution.py:185
  151.8 78.5 %layer.1 = bf16[512,256]{1,0:T(8,128)(2,1)} custom-call(bf16[2048,256]{1,0:T(8,128)(2,1)} %scatter_custom_fusion.3.points_ref, s32[1,2048]{1,0:T(1,128)} %bitcast.39, bf16[3,256,256]{2,1,0:T(8,128)(2,1)} %wqkv_ref.1, bf16[256,256]{1,0:T(8,128)(2,1)} %wout_ref.1, bf16[256,1024]{1,0:T(8,128)(2,1)} %wup_ref.1, bf16[1024,256]{1,0:T(8,128)(2,1)} %wdown_ref.1), custom_call_target="tpu_custom_call" | custom-call | tf_op jit(solution)/shard_map/layer/pallas_call | solution.py:143
  230.3 2.9 scatter_custom_fusion.4
  233.2 0.9 reshape.136
  234.1 0.0 all-to-all-done
  234.1 12.1 %all-to-all-start.6 = ((bf16[64,4,4,256]{3,2,1,0:T(4,128)(2,1)}), bf16[64,4,4,256]{3,2,1,0:T(4,128)(2,1)S(1)}, u32[]{:S(2)}, u32[]{:S(2)}) async-start(bf16[64,4,4,256]{3,2,1,0:T(4,128)(2,1)} %reshape.136), calls=%async_computation.6 | async-start | bytes 1048576 | tf_op jit(solution)/shard_map/all_to_all | solution.py:237
  246.2 0.1 copy.30
  246.3 0.7 reshape.202
  247.0 15.1 %all-to-all-done.6 = bf16[64,4,4,256]{3,2,1,0:T(4,128)(2,1)S(1)} async-done(((bf16[64,4,4,256]{3,2,1,0:T(4,128)(2,1)}), bf16[64,4,4,256]{3,2,1,0:T(4,128)(2,1)S(1)}, u32[]{:S(2)}, u32[]{:S(2)}) %all-to-all-start.6) | async-done | bytes 524320 | tf_op jit(solution)/shard_map/all_to_all | solution.py:237
  262.1 7.8 %all-to-all-start.1 = ((s32[4,1,256]{2,1,0:T(1,128)}), s32[4,1,256]{2,1,0:T(1,128)S(1)}, u32[]{:S(2)}, u32[]{:S(2)}) async-start(s32[4,1,256]{2,1,0:T(1,128)} %reshape.202), calls=%async_computation.1 | async-start | bytes 8192 | tf_op jit(solution)/shard_map/all_to_all | solution.py:243
  269.9 1.0 copy.39
  270.9 2.1 all-to-all-done.1
  273.0 4.1 %all-to-all-start.7 = ((bf16[64,4,4,256]{3,2,0,1:T(4,128)(2,1)}), bf16[64,4,4,256]{3,2,0,1:T(4,128)(2,1)S(1)}, u32[]{:S(2)}, u32[]{:S(2)}) async-start(bf16[64,4,4,256]{3,2,0,1:T(4,128)(2,1)} %copy.39), calls=%async_computation.7 | async-start | bytes 1048576 | tf_op jit(solution)/shard_map/all_to_all | solution.py:236
  277.2 0.6 reduce
  277.8 0.1 reshape.203
  277.8 0.1 copy.31
  278.0 0.2 reshape.129
  278.2 6.8 %all-to-all-done.7 = bf16[64,4,4,256]{3,2,0,1:T(4,128)(2,1)S(1)} async-done(((bf16[64,4,4,256]{3,2,0,1:T(4,128)(2,1)}), bf16[64,4,4,256]{3,2,0,1:T(4,128)(2,1)S(1)}, u32[]{:S(2)}, u32[]{:S(2)}) %all-to-all-start.7) | async-done | bytes 524320 | tf_op jit(solution)/shard_map/all_to_all | solution.py:236
  285.0 0.2 copy.40
  285.2 0.1 reshape.182
  285.3 5.0 %scatter_custom_fusion.5 = bf16[512,256]{1,0:T(8,128)(2,1)S(1)} fusion(s32[1024]{0:T(1024)S(1)} %bitcast.45, bf16[1024,256]{1,0:T(8,128)(2,1)S(1)} %reshape.182, bf16[]{:T(256)} %constant.82.clone.1), kind=kCustom, calls=%fused_computation.32 | custom fusion | bytes 262146 | tf_op jit(solution)/shard_map/scatter | solution.py:185
  290.3 0.4 fusion.25
  290.7 0.2 multiply_reduce_fusion
  290.9 0.3 multiply_convert_fusion
  291.1 1.0 copy.41
  (21 shorter events, 0.2 us)
Async XLA Ops:
  0.0 290.3 %copy-start = (bf16[256,512]{1,0:T(8,128)(2,1)S(1)}, bf16[256,512]{1,0:T(8,128)(2,1)}, u32[]{:S(2)}) copy-start(bf16[256,512]{1,0:T(8,128)(2,1)} %param.17) | copy-start | bytes 786436
  12.6 30.4 %all-to-all-start.2 = ((s32[64,4,12]{2,1,0:T(4,128)}), s32[64,4,12]{2,1,0:T(4,128)S(1)}, u32[]{:S(2)}, u32[]{:S(2)}) async-start(s32[64,4,12]{2,1,0:T(4,128)} %reshape.131), calls=%async_computation.2 | async-start | bytes 262144 | tf_op jit(solution)/shard_map/all_to_all | solution.py:222
  43.0 58.1 %copy-start.3 = (s32[512]{0:T(512)S(1)}, s32[512]{0:T(512)}, u32[]{:S(2)}) copy-start(s32[512]{0:T(512)} %param.12) | copy-start | bytes 6148
  43.0 50.5 %all-to-all-start.4 = ((bf16[64,4,12,256]{3,1,2,0:T(4,128)(2,1)}), bf16[64,4,12,256]{3,1,2,0:T(4,128)(2,1)S(1)}, u32[]{:S(2)}, u32[]{:S(2)}) async-start(bf16[64,4,12,256]{3,1,2,0:T(4,128)(2,1)} %copy.36), calls=%async_computation.4 | async-start | bytes 3145728 | tf_op jit(solution)/shard_map/all_to_all | solution.py:215
  93.5 10.7 %all-to-all-start.3 = ((s32[4,1,768]{2,1,0:T(1,128)}), s32[4,1,768]{2,1,0:T(1,128)S(1)}, u32[]{:S(2)}, u32[]{:S(2)}) async-start(s32[4,1,768]{2,1,0:T(1,128)} %reshape.204), calls=%async_computation.3 | async-start | bytes 24576 | tf_op jit(solution)/shard_map/all_to_all | solution.py:221
  104.2 23.3 %all-to-all-start.5 = ((bf16[64,4,12,256]{3,0,2,1:T(8,128)(2,1)}), bf16[64,4,12,256]{3,0,2,1:T(8,128)(2,1)S(1)}, u32[]{:S(2)}, u32[]{:S(2)}) async-start(bf16[64,4,12,256]{3,0,2,1:T(8,128)(2,1)} %copy.37), calls=%async_computation.5 | async-start | bytes 3145728 | tf_op jit(solution)/shard_map/all_to_all | solution.py:214
  108.5 4.1 %copy-start.2 = (s32[2048]{0:T(1024)S(1)}, s32[2048]{0:T(1024)}, u32[]{:S(2)}) copy-start(s32[2048]{0:T(1024)} %param.11) | copy-start | bytes 24580
  127.5 5.6 %copy-start.1 = (bf16[64,4,12,256]{3,0,2,1:T(8,128)(2,1)}, bf16[64,4,12,256]{3,0,2,1:T(8,128)(2,1)S(1)}, u32[]{:S(2)}) copy-start(bf16[64,4,12,256]{3,0,2,1:T(8,128)(2,1)S(1)} %all-to-all-done.5) | copy-start | bytes 4718596
  127.5 106.5 %all-to-all-start = ((s32[64,4,4]{2,1,0:T(4,128)}), s32[64,4,4]{2,1,0:T(4,128)S(1)}, u32[]{:S(2)}, u32[]{:S(2)}) async-start(s32[64,4,4]{2,1,0:T(4,128)} %reshape.128), calls=%async_computation | async-start | bytes 262144 | tf_op jit(solution)/shard_map/all_to_all | solution.py:244
  234.1 28.0 %all-to-all-start.6 = ((bf16[64,4,4,256]{3,2,1,0:T(4,128)(2,1)}), bf16[64,4,4,256]{3,2,1,0:T(4,128)(2,1)S(1)}, u32[]{:S(2)}, u32[]{:S(2)}) async-start(bf16[64,4,4,256]{3,2,1,0:T(4,128)(2,1)} %reshape.136), calls=%async_computation.6 | async-start | bytes 1048576 | tf_op jit(solution)/shard_map/all_to_all | solution.py:237
  262.1 10.9 %all-to-all-start.1 = ((s32[4,1,256]{2,1,0:T(1,128)}), s32[4,1,256]{2,1,0:T(1,128)S(1)}, u32[]{:S(2)}, u32[]{:S(2)}) async-start(s32[4,1,256]{2,1,0:T(1,128)} %reshape.202), calls=%async_computation.1 | async-start | bytes 8192 | tf_op jit(solution)/shard_map/all_to_all | solution.py:243
  273.0 12.0 %all-to-all-start.7 = ((bf16[64,4,4,256]{3,2,0,1:T(4,128)(2,1)}), bf16[64,4,4,256]{3,2,0,1:T(4,128)(2,1)S(1)}, u32[]{:S(2)}, u32[]{:S(2)}) async-start(bf16[64,4,4,256]{3,2,0,1:T(4,128)(2,1)} %copy.39), calls=%async_computation.7 | async-start | bytes 1048576 | tf_op jit(solution)/shard_map/all_to_all | solution.py:236
where the time goes:
time: 293 us; the launch traced here: 292 us
  Pallas kernels  78.5 us (27%)
  waiting for transfers between devices  75.5 us (26%)
  starting transfers between devices  68.9 us (24%)
  local copies, waits for them, and re-layouts  63.4 us (22%)
  other arithmetic  5.11 us (2%)
    pallas_call x1, Pallas kernels, layer(): pl.pallas_call(layer_kernel, out_shape=jax.ShapeDtypeStruct((voxels, widt...  78.5 us
    all_to_all x1, waiting for transfers between devices, per_device(): lax.all_to_all(packed, 'sp', split_axis=0, concat_axis=0, tiled=True)  37.4 us
    scatter x2, local copies, waits for them, and re-layouts, place_rows(): return jnp.zeros((block_len, arrived.shape[1]), arrived.dtype).at[slot_id...  19.9 us
    all_to_all x1, starting transfers between devices, per_device(): lax.all_to_all(slot_ids, 'sp', split_axis=0, concat_axis=0, tiled=True)  15.1 us
    all_to_all x1, waiting for transfers between devices, per_device(): lax.all_to_all(sent_rows, 'sp', split_axis=0, concat_axis=0, tiled=True)  15.1 us
    scatter x2, local copies, waits for them, and re-layouts, pack_rows(): packed = jnp.zeros((peer_count * capacity, row_data.shape[1]), row_data.d...  13.9 us
    all_to_all x1, waiting for transfers between devices, per_device(): lax.all_to_all(lax.all_to_all(packed, 'sp', split_axis=0, concat_axis=0,...  12.8 us
    all_to_all x1, starting transfers between devices, per_device(): lax.all_to_all(packed, 'sp', split_axis=0, concat_axis=0, tiled=True)  12.3 us
  transfers between devices with their start and end apart: 8, of which 6 were waited for; matrix products, arithmetic and copies ran while one was open for 17% of the time, Pallas kernels for 27%

commit v1 on v0

--- a/solution.py
+++ b/solution.py
@@ -159,117 +159,340 @@
     )(points, ids, w_qkv, w_out, w_up, w_down)
 
 
-def pack_rows(row_data, target, block_len, peer_count, capacity):
-    owner_block = target // block_len
-    slot_number = target % block_len
-    onehot = (owner_block[:, None] == jnp.arange(peer_count, dtype=jnp.int32)[None, :]).astype(
-        jnp.int32
+PLANES = 8
+SIDE = 32
+DEVS = PLANES * SIDE
+MESH = pl.DeviceIdType.MESH
+
+
+def turn(q):
+    sign = 1 - 2 * (q % 2)
+    return (PLANES + sign * (PLANES // 2 - q // 2)) % PLANES * ((q + PLANES - 1) // PLANES)
+
+
+class Links:
+    def __init__(self, inner):
+        self.inner = inner
+        me = lax.axis_index("sp") * inner + lax.axis_index("hd")
+        self.plane = me // SIDE
+        self.spot = me % SIDE
+
+    def at(self, plane, spot):
+        device = plane * SIDE + spot
+        return (device // self.inner, device % self.inner)
+
+    def above(self, k):
+        return self.at((self.plane + k) % PLANES, self.spot)
+
+    def beside(self, j):
+        return self.at(self.plane, (self.spot + j) % SIDE)
+
+    def greet(self):
+        barrier = pltpu.get_barrier_semaphore()
+
+        def up(k, c):
+            pl.semaphore_signal(barrier, inc=1, device_id=self.above(k), device_id_type=MESH)
+            return c
+
+        def side(j, c):
+            pl.semaphore_signal(barrier, inc=1, device_id=self.beside(j), device_id_type=MESH)
+            return c
+
+        lax.fori_loop(1, PLANES, up, 0)
+        lax.fori_loop(1, SIDE, side, 0)
+
+    def meet(self, ready):
+        pl.semaphore_wait(pltpu.get_barrier_semaphore(), PLANES - 1 + SIDE - 1)
+
+        def up(k, c):
+            pl.semaphore_signal(ready, inc=1, device_id=self.above(k), device_id_type=MESH)
+            return c
+
+        lax.fori_loop(1, PLANES, up, 0)
+
+    def send_all(self, streams, ready):
+        def one(k, j):
+            to = ((self.plane + k) % PLANES, (self.spot + j) % SIDE)
+            device = self.at(*to)
+            for source, target, sent, got in streams:
+                pltpu.make_async_remote_copy(
+                    source.at[to], target.at[self.plane, self.spot], sent.at[k], got.at[k],
+                    device_id=device, device_id_type=MESH,
+                ).start()
+
+        def near(j, c):
+            one(0, j)
+            return c
+
+        lax.fori_loop(1, SIDE, near, 0)
+        pl.semaphore_wait(ready, PLANES - 1)
+
+        def far(n, c):
+            one(turn(1 + n // SIDE), n % SIDE)
+            return c
+
+        lax.fori_loop(0, (PLANES - 1) * SIDE, far, 0)
+        for source, target, _, _ in streams:
+            target[self.plane, self.spot] = source[self.plane, self.spot]
+
+    def arrived(self, streams, k, count):
+        source = (self.plane + PLANES - k) % PLANES
+        for _, target, sent, got in streams:
+            held = target.at[source, pl.ds(0, count)]
+            pltpu.make_async_copy(held, held, sent.at[k]).wait()
+            pltpu.make_async_copy(held, held, got.at[k]).wait()
+        return source
+
+
+def rank_rows(target_ref, key_ref, block, full):
+    step = 256
+    sub = lax.broadcasted_iota(I32, (DEVS, step), 0)
+    lane = lax.broadcasted_iota(I32, (DEVS, step), 1)
+    before = jnp.where(sub < lane, 1.0, 0.0).astype(BF)
+    rep = lax.broadcasted_iota(I32, (128, step), 0) % 8
+    nt = (((1,), (1,)), ((), ()))
+
+    def ranks(b, carry):
+        seen, *sums = carry
+        r0 = pl.multiple_of(b * step, step)
+        target = target_ref[:, pl.ds(r0, step)]
+        owner = target // block
+        tag = target - owner * block + 1
+        mark = jnp.where(sub == owner, 1.0, 0.0)
+        marks = mark.astype(BF)
+        prior = mm(marks, before) + seen
+        rank = jnp.sum(mark * prior, axis=0, keepdims=True).astype(I32)
+        key_ref[:, pl.ds(r0, step)] = owner * 16 + rank
+        high = (tag // 16).astype(F32)
+        low = (tag % 16).astype(F32)
+
+        def gather(values, position):
+            picked = jnp.where(rank == position, values, 0.0).astype(BF)
+            return lax.dot_general(marks, picked, nt, preferred_element_type=F32)
+
+        found = [gather(high, full + rep % 4), gather(low, full + rep % 4)]
+        if full:
+            found += [gather(high, rep), gather(low, rep)]
+        sums = [s + f for s, f in zip(sums, found)]
+        return (seen + jnp.sum(mark, axis=1, keepdims=True), *sums)
+
+    zero = jnp.zeros((DEVS, 128), F32)
+    count = target_ref.shape[1]
+    _, *sums = lax.fori_loop(
+        0, count // step, ranks, (jnp.zeros((DEVS, 1), F32),) + (zero,) * (4 if full else 2)
     )
-    before = jnp.cumsum(onehot, axis=0) - onehot
-    positions = owner_block * capacity + jnp.sum(before * onehot, axis=1)
-    packed = (
-        jnp.zeros((peer_count * capacity, row_data.shape[1]), row_data.dtype)
-        .at[positions]
-        .set(row_data)
+    tags = [(sums[i] * 16.0 + sums[i + 1]).astype(I32) for i in range(0, len(sums), 2)]
+    return tags
+
+
+def pack_rows(x_ref, key_ref, send_ref, full):
+    count, width = x_ref.shape
+    half = width // 2
+    tiles = send_ref.shape[2]
+    spots = lax.broadcasted_iota(I32, (256, count), 0)
+    first = lax.broadcasted_iota(I32, (SIDE, 8, half), 1) < 4
+
+    def pack(z, c):
+        base = z * SIDE
+
+        def rows_of(rank):
+            wanted = (base + spots // 8) * 16 + rank
+            picks = jnp.where(key_ref[...] == wanted, 1.0, 0.0).astype(BF)
+            rows = mm(picks, x_ref[...])
+            return rows[:, :half].reshape(SIDE, 8, half), rows[:, half:].reshape(SIDE, 8, half)
+
+        if full:
+            left, right = rows_of(spots % 8)
+            send_ref[z, :, 0] = left.astype(BF)
+            send_ref[z, :, 1] = right.astype(BF)
+        left, right = rows_of(full + spots % 4)
+        send_ref[z, :, tiles - 1] = jnp.where(first, left, right).astype(BF)
+        return c
+
+    lax.fori_loop(0, PLANES, pack, 0)
+
+
+def place_rows(got_ref, source, marks, out_ref, full):
+    block, width = out_ref.shape
+    half = width // 2
+    tiles = got_ref.shape[2]
+    chunk = min(block, 512)
+    first = lax.broadcasted_iota(I32, (SIDE, 8, half), 1) < 4
+    weights = []
+    if full:
+        left = got_ref[source, :, 0].astype(F32).reshape(256, half)
+        right = got_ref[source, :, 1].astype(F32).reshape(256, half)
+        weights.append(jnp.concatenate([left, right], axis=1).astype(BF))
+    mixed = got_ref[source, :, tiles - 1].astype(F32)
+    left = jnp.where(first, mixed, 0.0).reshape(256, half)
+    right = jnp.where(first, 0.0, mixed).reshape(256, half)
+    weights.append(jnp.concatenate([left, right], axis=1).astype(BF))
+    weights = jnp.concatenate(weights, axis=0)
+    rows = lax.broadcasted_iota(I32, (chunk, marks.shape[1]), 0) + 1
+
+    def some(i, c):
+        r0 = pl.multiple_of(i * chunk, chunk)
+        picks = jnp.where(marks == rows + r0, 1.0, 0.0).astype(BF)
+        at_rows = pl.ds(r0, chunk)
+        out_ref[at_rows, :] = (out_ref[at_rows, :].astype(F32) + mm(picks, weights)).astype(BF)
+        return c
+
+    lax.fori_loop(0, block // chunk, some, 0)
+
+
+def spread_kernel(
+    full, inner, voxels, x_ref, target_ref, owner_ref, out_ref, key_out, marks_out,
+    key_s, send_s, tags_s, got_s, seen_s, d_send, d_recv, t_send, t_recv, ready,
+):
+    links = Links(inner)
+    links.greet()
+    block = out_ref.shape[0]
+    second, first = rank_rows(target_ref, key_s, block, full)
+    (third,) = rank_rows(owner_ref, key_out, voxels, 0)
+    lane = lax.broadcasted_iota(I32, (DEVS, 128), 1) // 8
+    spot = links.spot % 16
+    tags = jnp.where(lane == spot, first + 4096 * second, 0)
+    tags = jnp.where(lane == (spot + 8) % 16, third, tags)
+    tags_s[...] = tags.reshape(PLANES, SIDE, 1, 128)
+    pack_rows(x_ref, key_s, send_s, full)
+    out_ref[...] = jnp.zeros_like(out_ref)
+    links.meet(ready)
+    streams = ((tags_s, seen_s, t_send, t_recv), (send_s, got_s, d_send, d_recv))
+    links.send_all(streams, ready)
+    low = lax.broadcasted_iota(I32, (1, 128), 1) < 64
+
+    def land(k, count):
+        source = links.arrived(streams, k, count)
+        points, later = [], []
+        for part in range(2):
+            a = jnp.sum(seen_s[source, part * 16 : part * 16 + 8], axis=0)
+            b = jnp.sum(seen_s[source, part * 16 + 8 : part * 16 + 16], axis=0)
+            points.append(jnp.where(low, a, b))
+            other = jnp.where(low, b, a)
+            later.append(jnp.concatenate([other[:, 64:], other[:, :64]], axis=1))
+        points = jnp.concatenate(points, axis=1)
+        marks_out[source] = jnp.concatenate(later, axis=1)
+        marks = jnp.concatenate([points % 4096, points // 4096], axis=1)
+        place_rows(got_s, source, marks, out_ref, full)
+
+    land(0, SIDE - 1)
+
+    def more(q, c):
+        land(turn(q), SIDE)
+        return c
+
+    lax.fori_loop(1, PLANES, more, 0)
+
+
+def spread(x, target, owner, capacity, inner):
+    count, width = x.shape
+    voxels = owner.shape[1]
+    vm = pl.BlockSpec(memory_space=pltpu.VMEM)
+    data = pltpu.VMEM((PLANES, SIDE, capacity // 4, 8, width // 2), BF)
+    tags = pltpu.VMEM((PLANES, SIDE, 1, 128), I32)
+    return pl.pallas_call(
+        functools.partial(spread_kernel, capacity - 4, inner, voxels),
+        out_shape=(
+            jax.ShapeDtypeStruct((count, width), BF),
+            jax.ShapeDtypeStruct((1, voxels), I32),
+            jax.ShapeDtypeStruct((PLANES, 1, 256), I32),
+        ),
+        in_specs=[vm] * 3,
+        out_specs=[vm] * 3,
+        scratch_shapes=[pltpu.VMEM((1, count), I32), data, tags, data, tags]
+        + [pltpu.SemaphoreType.DMA((PLANES,))] * 4
+        + [pltpu.SemaphoreType.REGULAR],
+        compiler_params=pltpu.CompilerParams(
+            collective_id=1, has_side_effects=True, vmem_limit_bytes=56 * 2**20
+        ),
+        name="spread",
+    )(x, target, owner)
+
+
+def gather_kernel(
+    inner, x_ref, key_ref, marks_ref, out_ref, send_s, got_s, d_send, d_recv, ready
+):
+    links = Links(inner)
+    links.greet()
+    pack_rows(x_ref, key_ref, send_s, 0)
+    out_ref[...] = jnp.zeros_like(out_ref)
+    links.meet(ready)
+    streams = ((send_s, got_s, d_send, d_recv),)
+    links.send_all(streams, ready)
+
+    def land(k, count):
+        source = links.arrived(streams, k, count)
+        place_rows(got_s, source, marks_ref[source], out_ref, 0)
+
+    land(0, SIDE - 1)
+
+    def more(q, c):
+        land(turn(q), SIDE)
+        return c
+
+    lax.fori_loop(1, PLANES, more, 0)
+
+
+def gather(x, key, marks, inner):
+    count, width = x.shape
+    vm = pl.BlockSpec(memory_space=pltpu.VMEM)
+    data = pltpu.VMEM((PLANES, SIDE, 1, 8, width // 2), BF)
+    return pl.pallas_call(
+        functools.partial(gather_kernel, inner),
+        out_shape=jax.ShapeDtypeStruct((count, width), BF),
+        in_specs=[vm] * 3,
+        out_specs=vm,
+        scratch_shapes=[data, data]
+        + [pltpu.SemaphoreType.DMA((PLANES,))] * 2
+        + [pltpu.SemaphoreType.REGULAR],
+        compiler_params=pltpu.CompilerParams(
+            collective_id=2, has_side_effects=True, vmem_limit_bytes=56 * 2**20
+        ),
+        name="gather",
+    )(x, key, marks)
+
+
+def finish_kernel(x_ref, w_ref, out_ref):
+    block = 128
+
+    def some(i, c):
+        rows = pl.ds(pl.multiple_of(i * block, block), block)
+        out_ref[rows, :] = gelu(normalize(mm(x_ref[rows, :], w_ref[...]))).astype(BF)
+        return c
+
+    lax.fori_loop(0, x_ref.shape[0] // block, some, 0)
+
+
+def finish(x, w):
+    vm = pl.BlockSpec(memory_space=pltpu.VMEM)
+    return pl.pallas_call(
+        finish_kernel,
+        out_shape=jax.ShapeDtypeStruct((x.shape[0], w.shape[1]), BF),
+        in_specs=[vm] * 2,
+        out_specs=vm,
+        name="finish",
+    )(x, w)
+
+
+def per_device(features, point_dest, cluster, owner_row, w_qkv, w_out, w_up, w_down, w_pool):
+    inner = lax.axis_size("hd")
+    voxels = owner_row.shape[0]
+    me = lax.axis_index("sp") * inner + lax.axis_index("hd")
+    points, key, marks = spread(
+        features, point_dest.reshape(1, -1), owner_row.reshape(1, -1), 12, inner
     )
-    slot_ids = (
-        jnp.full((peer_count * capacity,), block_len, jnp.int32).at[positions].set(slot_number)
-    )
-    return (packed, slot_ids)
-
-
-def place_rows(arrived, slot_ids, block_len):
-    return (
-        jnp.zeros((block_len, arrived.shape[1]), arrived.dtype)
-        .at[slot_ids]
-        .set(arrived, mode="drop")
-    )
-
-
-def pack_voxels(row_data, owner_row, voxel_local, outer_count, inner_count):
-    device_count = outer_count * inner_count
-    capacity = 2 * (voxel_local // device_count)
-    width = row_data.shape[1]
-    packed, slot_ids = pack_rows(row_data, owner_row, voxel_local, device_count, capacity)
-    return (
-        packed.reshape(outer_count, inner_count, capacity, width),
-        slot_ids.reshape(outer_count, inner_count, capacity),
-    )
-
-
-def per_device(features, point_dest, cluster, owner_row, w_qkv, w_out, w_up, w_down, w_pool):
-    local_points = features.shape[0]
-    model_width = features.shape[1]
-    voxel_local = owner_row.shape[0]
-    outer_count = lax.axis_size("sp")
-    inner_count = lax.axis_size("hd")
-    device_count = outer_count * inner_count
-    device_number = lax.axis_index("sp") * inner_count + lax.axis_index("hd")
-    base_rows = local_points // device_count
-    capacity = base_rows + base_rows // 2
-    packed, slot_ids = pack_rows(features, point_dest, local_points, device_count, capacity)
-    packed = packed.reshape(outer_count, inner_count, capacity, model_width)
-    slot_ids = slot_ids.reshape(outer_count, inner_count, capacity)
-    arrived, arrived_slots = (
-        lax.all_to_all(
-            lax.all_to_all(packed, "sp", split_axis=0, concat_axis=0, tiled=True),
-            "hd",
-            split_axis=1,
-            concat_axis=1,
-            tiled=True,
-        ),
-        lax.all_to_all(
-            lax.all_to_all(slot_ids, "sp", split_axis=0, concat_axis=0, tiled=True),
-            "hd",
-            split_axis=1,
-            concat_axis=1,
-            tiled=True,
-        ),
-    )
-    points = place_rows(arrived.reshape(-1, model_width), arrived_slots.reshape(-1), local_points)
-    local_ids = cluster - device_number * voxel_local
-    means = layer(
-        points, local_ids.reshape(1, local_points), w_qkv, w_out, w_up, w_down, voxel_local
-    )
-    sent_rows, sent_slots = pack_voxels(means, owner_row, voxel_local, outer_count, inner_count)
-    got_rows, got_slots = (
-        lax.all_to_all(
-            lax.all_to_all(sent_rows, "sp", split_axis=0, concat_axis=0, tiled=True),
-            "hd",
-            split_axis=1,
-            concat_axis=1,
-            tiled=True,
-        ),
-        lax.all_to_all(
-            lax.all_to_all(sent_slots, "sp", split_axis=0, concat_axis=0, tiled=True),
-            "hd",
-            split_axis=1,
-            concat_axis=1,
-            tiled=True,
-        ),
-    )
-    placed = place_rows(
-        got_rows.reshape(-1, means.shape[1]), got_slots.reshape(-1), voxel_local
-    )
-    projected = mm(placed, w_pool)
-    return gelu(normalize(projected)).astype(BF)
+    local_ids = (cluster - me * voxels).reshape(1, -1)
+    means = layer(points, local_ids, w_qkv, w_out, w_up, w_down, voxels)
+    return finish(gather(means, key, marks, inner), w_pool)
 
 
 def solution(mesh):
+    rows = P(("sp", "hd"), None)
+    line = P(("sp", "hd"))
     return jax.shard_map(
         per_device,
         mesh=mesh,
-        in_specs=(
-            P(("sp", "hd"), None),
-            P(("sp", "hd")),
-            P(("sp", "hd")),
-            P(("sp", "hd")),
-            P(),
-            P(),
-            P(),
-            P(),
-            P(),
-        ),
-        out_specs=P(("sp", "hd"), None),
+        in_specs=(rows, line, line, line, P(), P(), P(), P(), P()),
+        out_specs=rows,
         check_vma=False,
     )

time: 293 us -> 176 us (0.60)
  Pallas kernels: 78.5 us -> 174 us
  waiting for transfers between devices: 75.5 us -> 0 us
  starting transfers between devices: 68.9 us -> 0 us
  local copies, waits for them, and re-layouts: 63.4 us -> 0.7 us
  other arithmetic: 5.11 us -> 0.6 us
    pallas_call x0 -> x3, Pallas kernels: none -> 96 us  [the longest x1 65.7 us: spread(): pl.pallas_call(functools.partial(spread_kernel, capacity - 4, inner, voxe...]
    all_to_all x8 -> x0, waiting for transfers between devices: 75.5 us -> none  [the longest x1 37.4 us: per_device(): lax.all_to_all(packed, 'sp', split_axis=0, concat_axis=0, tiled=True)]
    all_to_all x8 -> x0, starting transfers between devices: 68.9 us -> none  [the longest x1 15.1 us: per_device(): lax.all_to_all(slot_ids, 'sp', split_axis=0, concat_axis=0, tiled=True)]
    scatter x6 -> x0, local copies, waits for them, and re-layouts: 44.4 us -> none  [the longest x2 19.9 us: place_rows(): return jnp.zeros((block_len, arrived.shape[1]), arrived.dtype).at[slot_id...]
    reshape x9 -> x0, local copies, waits for them, and re-layouts: 8.73 us -> none  [the longest x2 4.31 us: per_device(): packed = packed.reshape(outer_count, inner_count, capacity, model_width)]
    all_to_all x9 -> x0, local copies, waits for them, and re-layouts: 6.15 us -> none  [the longest x1 2.34 us: per_device(): lax.all_to_all(lax.all_to_all(packed, 'sp', split_axis=0, concat_axis=0,...]
  transfers between devices with their start and end apart: 8 -> 0, of which waited for: 6 -> 0; matrix products, arithmetic and copies ran while one was open for 17% -> 0% of each run, Pallas kernels for 27% -> 0%
where the time goes in v1:
time: 176 us
  Pallas kernels  174 us (99%)
    pallas_call x1, Pallas kernels, layer(): pl.pallas_call(layer_kernel, out_shape=jax.ShapeDtypeStruct((voxels, widt...  78.5 us
    pallas_call x1, Pallas kernels, spread(): pl.pallas_call(functools.partial(spread_kernel, capacity - 4, inner, voxe...  65.7 us
    pallas_call x1, Pallas kernels, gather(): pl.pallas_call(functools.partial(gather_kernel, inner), out_shape=jax.Sha...  26.9 us

profile of v1, /device:TPU:1, one launch (start us, length us, event | category | flops | bytes accessed | tf_op | source)
XLA Modules:
  0.0 175.8 jit_solution(4676290921101154356)
XLA Ops:
  0.0 0.0 copy-start
  0.0 0.7 copy-done
  0.7 0.6 broadcast_subtract_fusion
  1.3 65.7 %spread.1 = (bf16[2048,256]{1,0:T(8,128)(2,1)}, s32[1,512]{1,0:T(1,128)}, s32[8,1,256]{2,1,0:T(1,128)}) custom-call(bf16[2048,256]{1,0:T(8,128)(2,1)} %x_ref.1, s32[1,2048]{1,0:T(1,128)} %bitcast.4, s32[1,512]{1,0:T(1,128)} %bitcast.5), custom_call_target="tpu_custom_call" | custom-call | tf_op jit(solution)/shard_map/spread/pallas_call | solution.py:393
  67.0 78.5 %layer.1.x_ref = bf16[512,256]{1,0:T(8,128)(2,1)} custom-call(bf16[2048,256]{1,0:T(8,128)(2,1)} %get-tuple-element.8.points_ref, s32[1,2048]{1,0:T(1,128)} %bitcast.3, bf16[3,256,256]{2,1,0:T(8,128)(2,1)} %wqkv_ref.1, bf16[256,256]{1,0:T(8,128)(2,1)} %wout_ref.1, bf16[256,1024]{1,0:T(8,128)(2,1)} %wup_ref.1, bf16[1024,256]{1,0:T(8,128)(2,1)} %wdown_ref.1), custom_call_target="tpu_custom_call" | custom-call | tf_op jit(solution)/shard_map/layer/pallas_call | solution.py:143
  145.5 26.9 %gather.1.x_ref = bf16[512,256]{1,0:T(8,128)(2,1)} custom-call(bf16[512,256]{1,0:T(8,128)(2,1)} %layer.1.x_ref, s32[1,512]{1,0:T(1,128)} %get-tuple-element.9.key_ref, s32[8,1,256]{2,1,0:T(1,128)} %get-tuple-element.10.marks_ref), custom_call_target="tpu_custom_call" | custom-call | tf_op jit(solution)/shard_map/gather/pallas_call | solution.py:440
  172.4 3.4 %finish.1 = bf16[512,512]{1,0:T(8,128)(2,1)} custom-call(bf16[512,256]{1,0:T(8,128)(2,1)} %gather.1.x_ref, bf16[256,512]{1,0:T(8,128)(2,1)} %w_ref.1), custom_call_target="tpu_custom_call" | custom-call | tf_op jit(solution)/shard_map/finish/pallas_call | solution.py:468
Async XLA Ops:
  0.0 0.7 copy-start

commit v2 on v1

v2 whole, which is shorter than its diff:
```python
import functools
import jax
import jax.numpy as jnp
from jax import lax
from jax.experimental import pallas as pl
from jax.experimental.pallas import tpu as pltpu
from jax.sharding import PartitionSpec as P

BF = jnp.bfloat16
F32 = jnp.float32
I32 = jnp.int32
HS = 16
PATCH = 1024
EPSILON = 1e-05
LOG2E = 1.4426950408889634
SCALE = HS ** (-0.5) * LOG2E
SAFE = 100.0


def normalize(values):
    center = jnp.mean(values, axis=-1, keepdims=True)
    shifted = values - center
    spread = jnp.mean(shifted * shifted, axis=-1, keepdims=True)
    return shifted * lax.rsqrt(spread + EPSILON)


def gelu(values):
    return 0.5 * values * (1.0 + lax.erf(values * (0.5**0.5)))


def mm(a, b):
    return jnp.dot(a, b, preferred_element_type=F32)


def attention_kernel(
    points_ref, wqkv_ref, att_ref, wq_s, wv_s, k_s, q_s, v_s,
):
    rows_all, width = points_ref.shape
    heads = width // HS
    blk = 256
    groups = width // 128
    wq_s[...] = wqkv_ref[0].T
    wv_s[...] = wqkv_ref[2].T
    v_s[:, HS:, :] = jnp.ones((heads, HS, PATCH), BF)
    head_mask = (
        lax.broadcasted_iota(I32, (width, 128), 0) // HS
        == lax.broadcasted_iota(I32, (width, 128), 1)
    ).astype(BF)

    def patch(number, carry):
        base = number * PATCH

        def project(i, bound):
            qmax, kmax = bound
            r0 = pl.multiple_of(i * blk, blk)
            x = points_ref[pl.ds(pl.multiple_of(base + r0, blk), blk), :].astype(F32)
            normed = normalize(x).astype(BF)
            keys = mm(normed, wqkv_ref[1])
            for g in range(groups):
                k_s[g, pl.ds(r0, blk), :] = keys[:, g * 128 : (g + 1) * 128].astype(BF)
            nt = (((1,), (1,)), ((), ()))
            queries = lax.dot_general(wq_s[...], normed, nt, preferred_element_type=F32)
            values = lax.dot_general(wv_s[...], normed, nt, preferred_element_type=F32)
            q_s[:, pl.ds(r0, blk)] = queries.astype(BF)
            v_s[:, 0:HS, pl.ds(r0, blk)] = values.astype(BF).reshape(heads, HS, blk)
            knorm = mm((keys * keys).astype(BF), head_mask)
            qnorm = jnp.sum((queries * queries).reshape(heads, HS, blk), axis=1)
            return (jnp.maximum(qmax, qnorm), jnp.maximum(kmax, jnp.max(knorm, axis=0, keepdims=True)))

        qmax, kmax = lax.fori_loop(
            0, PATCH // blk, project,
            (jnp.zeros((heads, blk), F32), jnp.zeros((1, 128), F32)),
        )
        bound = 1.05 * SCALE * SCALE * jnp.max(qmax) * jnp.max(kmax)
        qb = 512
        sub = lax.broadcasted_iota(I32, (128, qb), 0) // HS

        def attend(shifted):
            def head(h, c):
                g = h // 8
                r0 = pl.multiple_of(h * HS, HS)
                for q0 in range(0, PATCH, qb):
                    q = q_s[pl.ds(r0, HS), q0 : q0 + qb]
                    q = jnp.concatenate([q] * 8, axis=0)
                    q = jnp.where(sub == h % 8, q, jnp.zeros_like(q))
                    scores = mm(k_s[g], q)
                    if shifted:
                        scores = scores - jnp.max(scores, axis=0, keepdims=True)
                    raised = jnp.exp2(scores * SCALE).astype(BF)
                    out = mm(v_s[h], raised)
                    att_ref[number, pl.ds(r0, HS), q0 : q0 + qb] = (out[:HS] / out[HS : HS + 1]).astype(BF)
                return c

            lax.fori_loop(0, heads, head, 0)

        @pl.when(bound <= SAFE * SAFE)
        def _():
            attend(False)

        @pl.when(jnp.logical_not(bound <= SAFE * SAFE))
        def _():
            attend(True)

        return carry

    lax.fori_loop(0, rows_all // PATCH, patch, 0)


def attention(points, w_qkv):
    rows, width = points.shape
    heads = width // HS
    vm = pl.BlockSpec(memory_space=pltpu.VMEM)
    return pl.pallas_call(
        attention_kernel,
        out_shape=jax.ShapeDtypeStruct((rows // PATCH, width, PATCH), BF),
        in_specs=[vm] * 2,
        out_specs=vm,
        scratch_shapes=[
            pltpu.VMEM((width, width), BF),
            pltpu.VMEM((width, width), BF),
            pltpu.VMEM((width // 128, PATCH, 128), BF),
            pltpu.VMEM((width, PATCH), BF),
            pltpu.VMEM((heads, 2 * HS, PATCH), BF),
        ],
        compiler_params=pltpu.CompilerParams(vmem_limit_bytes=56 * 2**20),
        name="attention",
    )(points, w_qkv)


def tail(points_ref, att_ref, ids_ref, wout_ref, wup_ref, wdown_ref, fin_s, means_ref):
    rows_all = points_ref.shape[0]
    blk = 256
    per = PATCH // blk

    def mlp(i, c):
        rows = pl.ds(pl.multiple_of(i * blk, blk), blk)
        cols = pl.ds(pl.multiple_of(i % per * blk, blk), blk)
        attended = att_ref[i // per, :, cols].T
        middle = points_ref[rows, :].astype(F32) + mm(attended, wout_ref[...])
        normed = normalize(middle).astype(BF)
        hidden = gelu(mm(normed, wup_ref[...])).astype(BF)
        fin_s[rows, :] = (middle + mm(hidden, wdown_ref[...])).astype(BF)
        return c

    lax.fori_loop(0, rows_all // blk, mlp, 0)
    ids = ids_ref[...] - jnp.min(ids_ref[...], axis=1, keepdims=True)
    vb = 128

    def pool(i, c):
        v0 = pl.multiple_of(i * vb, vb)
        marks = jnp.where(lax.broadcasted_iota(I32, (vb, rows_all), 0) + v0 == ids, 1.0, 0.0)
        tally = jnp.sum(marks, axis=1, keepdims=True)
        means_ref[pl.ds(v0, vb), :] = (mm(marks.astype(BF), fin_s[...]) / tally).astype(BF)
        return c

    lax.fori_loop(0, means_ref.shape[0] // vb, pool, 0)


PLANES = 8
SIDE = 32
DEVS = PLANES * SIDE
GROUPS = DEVS // SIDE
MESH = pl.DeviceIdType.MESH


class Links:
    def __init__(self, inner):
        self.inner = inner
        me = lax.axis_index("sp") * inner + lax.axis_index("hd")
        self.plane = lax.div(me, SIDE)
        self.spot = lax.rem(me, SIDE)

    def peer(self, k, j):
        return lax.rem(self.plane + k, PLANES), lax.rem(self.spot + j, SIDE)

    def device(self, plane, spot):
        number = plane * SIDE + spot
        return lax.div(number, self.inner), lax.rem(number, self.inner)

    def signal(self, sem, k, j):
        pl.semaphore_signal(
            sem, inc=1, device_id=self.device(*self.peer(k, j)), device_id_type=MESH
        )

    def greet(self):
        barrier = pltpu.get_barrier_semaphore()

        def up(k, c):
            self.signal(barrier, k, 0)
            return c

        def side(j, c):
            self.signal(barrier, 0, j)
            return c

        lax.fori_loop(1, PLANES, up, 0)
        lax.fori_loop(1, SIDE, side, 0)

    def pass_on(self, ready):
        pl.semaphore_wait(pltpu.get_barrier_semaphore(), PLANES - 1 + SIDE - 1)

        def up(k, c):
            self.signal(ready, k, 0)
            return c

        lax.fori_loop(1, PLANES, up, 0)

    def send(self, streams, g, start):
        def one(s, c):
            plane, spot = self.peer(
                lax.rem(s, PLANES), g * (SIDE // PLANES) + lax.div(s, PLANES)
            )
            for source, by_device, target, sent, got in streams:
                pltpu.make_async_remote_copy(
                    source.at[plane, spot] if by_device else source.at[g, s],
                    target.at[g, s], sent.at[g], got.at[g],
                    device_id=self.device(plane, spot), device_id_type=MESH,
                ).start()
            return c

        lax.fori_loop(start, SIDE, one, 0)

    def keep(self, streams):
        for source, by_device, target, _, _ in streams:
            target[0, 0] = source[self.plane, self.spot] if by_device else source[0, 0]

    def send_all(self, data, pack, ready, extra=None, prepare=None):
        pack(0)
        self.pass_on(ready)
        pack(1)
        self.keep((data,))
        pl.semaphore_wait(ready, PLANES - 1)
        self.send((data,), 0, 1)
        self.send((data,), 1, 0)
        pack(2)
        streams = (data,)
        if extra is not None:
            prepare()
            self.keep((extra,))
            self.send((extra,), 0, 1)
            self.send((extra,), 1, 0)
            streams = (extra, data)

        def more(g, c):
            pack(g + 1)
            self.send(streams, g, 0)
            return c

        lax.fori_loop(2, GROUPS - 1, more, 0)
        self.send(streams, GROUPS - 1, 0)

    def arrived(self, streams, g, count):
        for _, _, target, sent, got in streams:
            held = target.at[g, pl.ds(0, count)]
            pltpu.make_async_copy(held, held, sent.at[g]).wait()
            pltpu.make_async_copy(held, held, got.at[g]).wait()


def rank_rows(target_ref, key_ref, block):
    step = 256
    sub = lax.broadcasted_iota(I32, (DEVS, step), 0)
    lane = lax.broadcasted_iota(I32, (DEVS, step), 1)
    before = jnp.where(sub < lane, 1.0, 0.0).astype(BF)
    count = target_ref.shape[1]

    def ranks(b, seen):
        cols = pl.ds(pl.multiple_of(b * step, step), step)
        owner = lax.shift_right_logical(target_ref[:, cols], block.bit_length() - 1)
        mark = jnp.where(sub == owner, 1.0, 0.0)
        prior = mm(mark.astype(BF), before) + seen
        rank = jnp.sum(mark * prior, axis=0, keepdims=True).astype(I32)
        key_ref[:, cols] = owner * 16 + rank
        return seen + jnp.sum(mark, axis=1, keepdims=True)

    lax.fori_loop(0, count // step, ranks, jnp.zeros((DEVS, 1), F32))


def tag_rows(target_ref, key_ref, acc_ref, block, ranks):
    step = 256
    sub = lax.broadcasted_iota(I32, (DEVS, step), 0)
    nt = (((1,), (1,)), ((), ()))
    width = 256 * len(ranks)
    acc_ref[:, :width] = jnp.zeros((DEVS, width), F32)

    def some(b, c):
        cols = pl.ds(pl.multiple_of(b * step, step), step)
        key = key_ref[:, cols]
        rank = key & 15
        tag = (target_ref[:, cols] & (block - 1)) + 1
        high = lax.shift_right_logical(tag, 4).astype(F32)
        low = (tag & 15).astype(F32)
        marks = jnp.where(sub == lax.shift_right_logical(key, 4), 1.0, 0.0).astype(BF)
        picked = [
            jnp.where(rank == wanted, part, 0.0).astype(BF)
            for wanted in ranks
            for part in (high, low)
        ]
        picked = jnp.concatenate(picked, axis=0)
        acc_ref[:, :width] += lax.dot_general(marks, picked, nt, preferred_element_type=F32)
        return c

    lax.fori_loop(0, target_ref.shape[1] // step, some, 0)
    return [
        (acc_ref[:, i : i + 128] * 16.0 + acc_ref[:, i + 128 : i + 256]).astype(I32)
        for i in range(0, width, 256)
    ]


def packer(links, x_ref, key_ref, send_ref, full):
    width = x_ref.shape[1]
    half = width // 2
    tiles = send_ref.shape[2]
    column = lax.broadcasted_iota(I32, (256, 1), 0)
    slot = lax.shift_right_logical(column, 3)
    rank = column & 7
    first = lax.broadcasted_iota(I32, (SIDE, 8, half), 1) < 4

    def pack(g):
        plane = (links.plane + (slot & (PLANES - 1))) & (PLANES - 1)
        spot = (links.spot + g * (SIDE // PLANES) + lax.shift_right_logical(slot, 3)) & (SIDE - 1)
        base = (plane * SIDE + spot) * 16

        def rows_of(wanted):
            picks = jnp.where(key_ref[...] == wanted, 1.0, 0.0).astype(BF)
            rows = mm(picks, x_ref[...])
            return rows[:, :half].reshape(SIDE, 8, half), rows[:, half:].reshape(SIDE, 8, half)

        if full:
            left, right = rows_of(base + rank)
            send_ref[g, :, 0] = left.astype(BF)
            send_ref[g, :, 1] = right.astype(BF)
        left, right = rows_of(base + full + (rank & 3))
        send_ref[g, :, tiles - 1] = jnp.where(first, left, right).astype(BF)

    return pack


def place_rows(got_ref, g, marks, out_ref, full):
    block, width = out_ref.shape
    half = width // 2
    tiles = got_ref.shape[2]
    chunk = min(block, 512)
    first = lax.broadcasted_iota(I32, (SIDE, 8, half), 1) < 4
    weights = []
    if full:
        left = got_ref[g, :, 0].astype(F32).reshape(256, half)
        right = got_ref[g, :, 1].astype(F32).reshape(256, half)
        weights.append(jnp.concatenate([left, right], axis=1).astype(BF))
    mixed = got_ref[g, :, tiles - 1].astype(F32)
    left = jnp.where(first, mixed, 0.0).reshape(256, half)
    right = jnp.where(first, 0.0, mixed).reshape(256, half)
    weights.append(jnp.concatenate([left, right], axis=1).astype(BF))
    weights = jnp.concatenate(weights, axis=0)
    rows = lax.broadcasted_iota(I32, (chunk, 1), 0) + 1

    def some(i, c):
        r0 = pl.multiple_of(i * chunk, chunk)
        picks = jnp.where(marks == rows + r0, 1.0, 0.0).astype(BF)
        at_rows = pl.ds(r0, chunk)
        out_ref[at_rows, :] = (out_ref[at_rows, :].astype(F32) + mm(picks, weights)).astype(BF)
        return c

    lax.fori_loop(0, block // chunk, some, 0)


def spread_kernel(
    full, inner, voxels, x_ref, target_ref, owner_ref, out_ref, key_out, marks_out,
    key_s, acc_s, send_s, tags_s, got_s, seen_s, d_send, d_recv, t_send, t_recv, ready,
):
    links = Links(inner)
    links.greet()
    block = out_ref.shape[0]
    rank_rows(target_ref, key_s, block)

    def prepare():
        rank_rows(owner_ref, key_out, voxels)
        eight = lax.broadcasted_iota(I32, (128, 1), 0) & 7
        four = eight & 3
        first, second = tag_rows(target_ref, key_s, acc_s, block, (eight, full + four))
        (third,) = tag_rows(owner_ref, key_out, acc_s, voxels, (four,))
        lane = lax.shift_right_logical(lax.broadcasted_iota(I32, (DEVS, 128), 1), 3)
        owner = lax.broadcasted_iota(I32, (DEVS, 1), 0)
        k = (lax.shift_right_logical(owner, 5) - links.plane) & (PLANES - 1)
        j = ((owner & (SIDE - 1)) - links.spot) & (SIDE - 1)
        slot = (j & 1) * 8 + k
        tags = jnp.where(lane == slot, first + 4096 * second, 0)
        tags = jnp.where(lane == (slot + 8) & 15, third, tags)
        tags_s[...] = tags.reshape(PLANES, SIDE, 1, 128)
        out_ref[...] = jnp.zeros_like(out_ref)

    extra = (tags_s, True, seen_s, t_send, t_recv)
    data = (send_s, False, got_s, d_send, d_recv)
    links.send_all(data, packer(links, x_ref, key_s, send_s, full), ready, extra, prepare)
    streams = (extra, data)
    low = lax.broadcasted_iota(I32, (1, 128), 1) < 64

    def land(g, count):
        links.arrived(streams, g, count)
        points, later = [], []
        for part in range(2):
            a = jnp.sum(seen_s[g, part * 16 : part * 16 + 8], axis=0)
            b = jnp.sum(seen_s[g, part * 16 + 8 : part * 16 + 16], axis=0)
            points.append(jnp.where(low, a, b))
            other = jnp.where(low, b, a)
            later.append(jnp.concatenate([other[:, 64:], other[:, :64]], axis=1))
        points = jnp.concatenate(points, axis=1)
        marks_out[g] = jnp.concatenate(later, axis=1)
        marks = jnp.concatenate(
            [points & 4095, lax.shift_right_logical(points, 12)], axis=1
        )
        place_rows(got_s, g, marks, out_ref, full)

    land(0, SIDE - 1)

    def more(g, c):
        land(g, SIDE)
        return c

    lax.fori_loop(1, GROUPS, more, 0)


def spread(x, target, owner, capacity, inner):
    count, width = x.shape
    voxels = owner.shape[1]
    vm = pl.BlockSpec(memory_space=pltpu.VMEM)
    data = pltpu.VMEM((PLANES, SIDE, capacity // 4, 8, width // 2), BF)
    tags = pltpu.VMEM((PLANES, SIDE, 1, 128), I32)
    return pl.pallas_call(
        functools.partial(spread_kernel, capacity - 4, inner, voxels),
        out_shape=(
            jax.ShapeDtypeStruct((count, width), BF),
            jax.ShapeDtypeStruct((1, voxels), I32),
            jax.ShapeDtypeStruct((PLANES, 1, 256), I32),
        ),
        in_specs=[vm] * 3,
        out_specs=[vm] * 3,
        scratch_shapes=[
            pltpu.VMEM((1, count), I32), pltpu.VMEM((DEVS, 512), F32), data, tags, data, tags
        ]
        + [pltpu.SemaphoreType.DMA((PLANES,))] * 4
        + [pltpu.SemaphoreType.REGULAR],
        compiler_params=pltpu.CompilerParams(
            collective_id=1, has_side_effects=True, vmem_limit_bytes=56 * 2**20
        ),
        name="spread",
    )(x, target, owner)


def gather_kernel(
    inner, points_ref, att_ref, ids_ref, wout_ref, wup_ref, wdown_ref, key_ref, marks_ref, out_ref,
    fin_s, x_ref, send_s, got_s, d_send, d_recv, ready,
):
    links = Links(inner)
    links.greet()
    tail(points_ref, att_ref, ids_ref, wout_ref, wup_ref, wdown_ref, fin_s, x_ref)
    out_ref[...] = jnp.zeros_like(out_ref)
    data = (send_s, False, got_s, d_send, d_recv)
    links.send_all(data, packer(links, x_ref, key_ref, send_s, 0), ready)
    streams = (data,)

    def land(g, count):
        links.arrived(streams, g, count)
        place_rows(got_s, g, marks_ref[g], out_ref, 0)

    land(0, SIDE - 1)

    def more(g, c):
        land(g, SIDE)
        return c

    lax.fori_loop(1, GROUPS, more, 0)


def gather(points, att, ids, w_out, w_up, w_down, key, marks, inner):
    width = points.shape[1]
    count = key.shape[1]
    vm = pl.BlockSpec(memory_space=pltpu.VMEM)
    data = pltpu.VMEM((PLANES, SIDE, 1, 8, width // 2), BF)
    return pl.pallas_call(
        functools.partial(gather_kernel, inner),
        out_shape=jax.ShapeDtypeStruct((count, width), BF),
        in_specs=[vm] * 8,
        out_specs=vm,
        scratch_shapes=[pltpu.VMEM(points.shape, BF), pltpu.VMEM((count, width), BF), data, data]
        + [pltpu.SemaphoreType.DMA((PLANES,))] * 2
        + [pltpu.SemaphoreType.REGULAR],
        compiler_params=pltpu.CompilerParams(
            collective_id=2, has_side_effects=True, vmem_limit_bytes=56 * 2**20
        ),
        name="gather",
    )(points, att, ids, w_out, w_up, w_down, key, marks)


def finish_kernel(x_ref, w_ref, out_ref):
    block = 128

    def some(i, c):
        rows = pl.ds(pl.multiple_of(i * block, block), block)
        out_ref[rows, :] = gelu(normalize(mm(x_ref[rows, :], w_ref[...]))).astype(BF)
        return c

    lax.fori_loop(0, x_ref.shape[0] // block, some, 0)


def finish(x, w):
    vm = pl.BlockSpec(memory_space=pltpu.VMEM)
    return pl.pallas_call(
        finish_kernel,
        out_shape=jax.ShapeDtypeStruct((x.shape[0], w.shape[1]), BF),
        in_specs=[vm] * 2,
        out_specs=vm,
        name="finish",
    )(x, w)


def per_device(features, point_dest, cluster, owner_row, w_qkv, w_out, w_up, w_down, w_pool):
    inner = lax.axis_size("hd")
    points, key, marks = spread(
        features, point_dest.reshape(1, -1), owner_row.reshape(1, -1), 12, inner
    )
    att = attention(points, w_qkv)
    placed = gather(
        points, att, cluster.reshape(1, -1), w_out, w_up, w_down, key, marks, inner
    )
    return finish(placed, w_pool)


def solution(mesh):
    rows = P(("sp", "hd"), None)
    line = P(("sp", "hd"))
    return jax.shard_map(
        per_device,
        mesh=mesh,
        in_specs=(rows, line, line, line, P(), P(), P(), P(), P()),
        out_specs=rows,
        check_vma=False,
    )
```

time: 176 us -> 161 us (0.915)
  Pallas kernels: 174 us -> 161 us
    pallas_call x1, Pallas kernels: 65.7 us -> 56.3 us  [spread(): pl.pallas_call(functools.partial(spread_kernel, capacity - 4, inner, voxe...]
    pallas_call x1, Pallas kernels: 78.5 us -> 69.8 us  [attention(): pl.pallas_call(attention_kernel, out_shape=jax.ShapeDtypeStruct((rows //...]
    pallas_call x1, Pallas kernels: 26.9 us -> 31.1 us  [gather(): pl.pallas_call(functools.partial(gather_kernel, inner), out_shape=jax.Sha...]
where the time goes in v2:
time: 161 us
  Pallas kernels  161 us (100%)
    pallas_call x1, Pallas kernels, attention(): pl.pallas_call(attention_kernel, out_shape=jax.ShapeDtypeStruct((rows //...  69.8 us
    pallas_call x1, Pallas kernels, spread(): pl.pallas_call(functools.partial(spread_kernel, capacity - 4, inner, voxe...  56.3 us
    pallas_call x1, Pallas kernels, gather(): pl.pallas_call(functools.partial(gather_kernel, inner), out_shape=jax.Sha...  31.1 us
    pallas_call x1, Pallas kernels, finish(): pl.pallas_call(finish_kernel, out_shape=jax.ShapeDtypeStruct((x.shape[0],...  3.39 us

profile of v2, /device:TPU:1, one launch (start us, length us, event | category | flops | bytes accessed | tf_op | source)
XLA Modules:
  0.0 160.7 jit_solution(2293936989521811900)
XLA Ops:
  0.0 56.3 %spread.1 = (bf16[2048,256]{1,0:T(8,128)(2,1)}, s32[1,512]{1,0:T(1,128)}, s32[8,1,256]{2,1,0:T(1,128)}) custom-call(bf16[2048,256]{1,0:T(8,128)(2,1)} %x_ref.1, s32[1,2048]{1,0:T(1,128)} %bitcast.3, s32[1,512]{1,0:T(1,128)} %bitcast.5), custom_call_target="tpu_custom_call" | custom-call | tf_op jit(solution)/shard_map/spread/pallas_call | solution.py:428
  56.4 69.8 %attention.1.att_ref = bf16[2,256,1024]{2,1,0:T(8,128)(2,1)} custom-call(bf16[2048,256]{1,0:T(8,128)(2,1)} %get-tuple-element.8.points_ref, bf16[3,256,256]{2,1,0:T(8,128)(2,1)} %wqkv_ref.1), custom_call_target="tpu_custom_call" | custom-call | tf_op jit(solution)/shard_map/attention/pallas_call | solution.py:113
  126.1 31.1 %gather.1.x_ref = bf16[512,256]{1,0:T(8,128)(2,1)} custom-call(bf16[2048,256]{1,0:T(8,128)(2,1)} %get-tuple-element.8.points_ref, bf16[2,256,1024]{2,1,0:T(8,128)(2,1)} %attention.1.att_ref, s32[1,2048]{1,0:T(1,128)} %bitcast.4, bf16[256,256]{1,0:T(8,128)(2,1)} %wout_ref.1, bf16[256,1024]{1,0:T(8,128)(2,1)} %wup_ref.1, bf16[1024,256]{1,0:T(8,128)(2,1)} %wdown_ref.1, ...), custom_call_target="tpu_custom_call" | custom-call | tf_op jit(solution)/shard_map/gather/pallas_call | solution.py:479
  157.3 3.4 %finish.1 = bf16[512,512]{1,0:T(8,128)(2,1)} custom-call(bf16[512,256]{1,0:T(8,128)(2,1)} %gather.1.x_ref, bf16[256,512]{1,0:T(8,128)(2,1)} %w_ref.1), custom_call_target="tpu_custom_call" | custom-call | tf_op jit(solution)/shard_map/finish/pallas_call | solution.py:507

commit v3 on v2

--- a/solution.py
+++ b/solution.py
@@ -70,6 +70,7 @@
         qmax, kmax = lax.fori_loop(
             0, PATCH // blk, project,
             (jnp.zeros((heads, blk), F32), jnp.zeros((1, 128), F32)),
+            unroll=2,
         )
         bound = 1.05 * SCALE * SCALE * jnp.max(qmax) * jnp.max(kmax)
         qb = 512
@@ -91,7 +92,7 @@
                     att_ref[number, pl.ds(r0, HS), q0 : q0 + qb] = (out[:HS] / out[HS : HS + 1]).astype(BF)
                 return c
 
-            lax.fori_loop(0, heads, head, 0)
+            lax.fori_loop(0, heads, head, 0, unroll=1 if shifted else 2)
 
         @pl.when(bound <= SAFE * SAFE)
         def _():
@@ -142,7 +143,7 @@
         fin_s[rows, :] = (middle + mm(hidden, wdown_ref[...])).astype(BF)
         return c
 
-    lax.fori_loop(0, rows_all // blk, mlp, 0)
+    lax.fori_loop(0, rows_all // blk, mlp, 0, unroll=2)
     ids = ids_ref[...] - jnp.min(ids_ref[...], axis=1, keepdims=True)
     vb = 128
 
@@ -153,7 +154,7 @@
         means_ref[pl.ds(v0, vb), :] = (mm(marks.astype(BF), fin_s[...]) / tally).astype(BF)
         return c
 
-    lax.fori_loop(0, means_ref.shape[0] // vb, pool, 0)
+    lax.fori_loop(0, means_ref.shape[0] // vb, pool, 0, unroll=2)
 
 
 PLANES = 8

time: 161 us -> 158 us (0.981)
  Pallas kernels: 161 us -> 158 us
    pallas_call x1, Pallas kernels: 31.1 us -> 29.2 us  [gather(): pl.pallas_call(functools.partial(gather_kernel, inner), out_shape=jax.Sha...]
where the time goes in v3:
time: 158 us
  Pallas kernels  158 us (100%)
    pallas_call x1, Pallas kernels, attention(): pl.pallas_call(attention_kernel, out_shape=jax.ShapeDtypeStruct((rows //...  68.6 us
    pallas_call x1, Pallas kernels, spread(): pl.pallas_call(functools.partial(spread_kernel, capacity - 4, inner, voxe...  56.3 us
    pallas_call x1, Pallas kernels, gather(): pl.pallas_call(functools.partial(gather_kernel, inner), out_shape=jax.Sha...  29.2 us
    pallas_call x1, Pallas kernels, finish(): pl.pallas_call(finish_kernel, out_shape=jax.ShapeDtypeStruct((x.shape[0],...  3.39 us

profile of v3, /device:TPU:1, one launch (start us, length us, event | category | flops | bytes accessed | tf_op | source)
XLA Modules:
  0.0 157.6 jit_solution(1527997890797437215)
XLA Ops:
  0.0 56.3 %spread.1 = (bf16[2048,256]{1,0:T(8,128)(2,1)}, s32[1,512]{1,0:T(1,128)}, s32[8,1,256]{2,1,0:T(1,128)}) custom-call(bf16[2048,256]{1,0:T(8,128)(2,1)} %x_ref.1, s32[1,2048]{1,0:T(1,128)} %bitcast.3, s32[1,512]{1,0:T(1,128)} %bitcast.5), custom_call_target="tpu_custom_call" | custom-call | tf_op jit(solution)/shard_map/spread/pallas_call | solution.py:429
  56.4 68.6 %attention.1.att_ref = bf16[2,256,1024]{2,1,0:T(8,128)(2,1)} custom-call(bf16[2048,256]{1,0:T(8,128)(2,1)} %get-tuple-element.8.points_ref, bf16[3,256,256]{2,1,0:T(8,128)(2,1)} %wqkv_ref.1), custom_call_target="tpu_custom_call" | custom-call | tf_op jit(solution)/shard_map/attention/pallas_call | solution.py:114
  125.0 29.2 %gather.1.x_ref = bf16[512,256]{1,0:T(8,128)(2,1)} custom-call(bf16[2048,256]{1,0:T(8,128)(2,1)} %get-tuple-element.8.points_ref, bf16[2,256,1024]{2,1,0:T(8,128)(2,1)} %attention.1.att_ref, s32[1,2048]{1,0:T(1,128)} %bitcast.4, bf16[256,256]{1,0:T(8,128)(2,1)} %wout_ref.1, bf16[256,1024]{1,0:T(8,128)(2,1)} %wup_ref.1, bf16[1024,256]{1,0:T(8,128)(2,1)} %wdown_ref.1, ...), custom_call_target="tpu_custom_call" | custom-call | tf_op jit(solution)/shard_map/gather/pallas_call | solution.py:480
  154.2 3.4 %finish.1 = bf16[512,512]{1,0:T(8,128)(2,1)} custom-call(bf16[512,256]{1,0:T(8,128)(2,1)} %gather.1.x_ref, bf16[256,512]{1,0:T(8,128)(2,1)} %w_ref.1), custom_call_target="tpu_custom_call" | custom-call | tf_op jit(solution)/shard_map/finish/pallas_call | solution.py:508

commit v4 on v3

--- a/solution.py
+++ b/solution.py
@@ -208,8 +208,9 @@
 
     def send(self, streams, g, start):
         def one(s, c):
+            b = lax.div(s, PLANES)
             plane, spot = self.peer(
-                lax.rem(s, PLANES), g * (SIDE // PLANES) + lax.div(s, PLANES)
+                lax.rem(s, PLANES), PLANES * b + lax.rem(g + 2 * b, PLANES)
             )
             for source, by_device, target, sent, got in streams:
                 pltpu.make_async_remote_copy(
@@ -318,7 +319,8 @@
 
     def pack(g):
         plane = (links.plane + (slot & (PLANES - 1))) & (PLANES - 1)
-        spot = (links.spot + g * (SIDE // PLANES) + lax.shift_right_logical(slot, 3)) & (SIDE - 1)
+        b = lax.shift_right_logical(slot, 3)
+        spot = (links.spot + PLANES * b + ((g + 2 * b) & (PLANES - 1))) & (SIDE - 1)
         base = (plane * SIDE + spot) * 16
 
         def rows_of(wanted):
@@ -383,7 +385,7 @@
         owner = lax.broadcasted_iota(I32, (DEVS, 1), 0)
         k = (lax.shift_right_logical(owner, 5) - links.plane) & (PLANES - 1)
         j = ((owner & (SIDE - 1)) - links.spot) & (SIDE - 1)
-        slot = (j & 1) * 8 + k
+        slot = (lax.shift_right_logical(j, 3) & 1) * 8 + k
         tags = jnp.where(lane == slot, first + 4096 * second, 0)
         tags = jnp.where(lane == (slot + 8) & 15, third, tags)
         tags_s[...] = tags.reshape(PLANES, SIDE, 1, 128)

time: 158 us -> 159 us (level)
  no operation moved by 1% of the time
where the time goes in v4:
time: 159 us
  Pallas kernels  159 us (100%)
    pallas_call x1, Pallas kernels, attention(): pl.pallas_call(attention_kernel, out_shape=jax.ShapeDtypeStruct((rows //...  68.6 us
    pallas_call x1, Pallas kernels, spread(): pl.pallas_call(functools.partial(spread_kernel, capacity - 4, inner, voxe...  57 us
    pallas_call x1, Pallas kernels, gather(): pl.pallas_call(functools.partial(gather_kernel, inner), out_shape=jax.Sha...  29.5 us
    pallas_call x1, Pallas kernels, finish(): pl.pallas_call(finish_kernel, out_shape=jax.ShapeDtypeStruct((x.shape[0],...  3.39 us

profile of v4, /device:TPU:1, one launch (start us, length us, event | category | flops | bytes accessed | tf_op | source)
XLA Modules:
  0.0 158.5 jit_solution(2433084729350165222)
XLA Ops:
  0.0 57.0 %spread.1 = (bf16[2048,256]{1,0:T(8,128)(2,1)}, s32[1,512]{1,0:T(1,128)}, s32[8,1,256]{2,1,0:T(1,128)}) custom-call(bf16[2048,256]{1,0:T(8,128)(2,1)} %x_ref.1, s32[1,2048]{1,0:T(1,128)} %bitcast.3, s32[1,512]{1,0:T(1,128)} %bitcast.5), custom_call_target="tpu_custom_call" | custom-call | tf_op jit(solution)/shard_map/spread/pallas_call | solution.py:431
  57.0 68.6 %attention.1.att_ref = bf16[2,256,1024]{2,1,0:T(8,128)(2,1)} custom-call(bf16[2048,256]{1,0:T(8,128)(2,1)} %get-tuple-element.8.points_ref, bf16[3,256,256]{2,1,0:T(8,128)(2,1)} %wqkv_ref.1), custom_call_target="tpu_custom_call" | custom-call | tf_op jit(solution)/shard_map/attention/pallas_call | solution.py:114
  125.6 29.5 %gather.1.x_ref = bf16[512,256]{1,0:T(8,128)(2,1)} custom-call(bf16[2048,256]{1,0:T(8,128)(2,1)} %get-tuple-element.8.points_ref, bf16[2,256,1024]{2,1,0:T(8,128)(2,1)} %attention.1.att_ref, s32[1,2048]{1,0:T(1,128)} %bitcast.4, bf16[256,256]{1,0:T(8,128)(2,1)} %wout_ref.1, bf16[256,1024]{1,0:T(8,128)(2,1)} %wup_ref.1, bf16[1024,256]{1,0:T(8,128)(2,1)} %wdown_ref.1, ...), custom_call_target="tpu_custom_call" | custom-call | tf_op jit(solution)/shard_map/gather/pallas_call | solution.py:482
  155.1 3.4 %finish.1 = bf16[512,512]{1,0:T(8,128)(2,1)} custom-call(bf16[512,256]{1,0:T(8,128)(2,1)} %gather.1.x_ref, bf16[256,512]{1,0:T(8,128)(2,1)} %w_ref.1), custom_call_target="tpu_custom_call" | custom-call | tf_op jit(solution)/shard_map/finish/pallas_call | solution.py:510

commit v5 on v3

--- a/solution.py
+++ b/solution.py
@@ -92,7 +92,7 @@
                     att_ref[number, pl.ds(r0, HS), q0 : q0 + qb] = (out[:HS] / out[HS : HS + 1]).astype(BF)
                 return c
 
-            lax.fori_loop(0, heads, head, 0, unroll=1 if shifted else 2)
+            lax.fori_loop(0, heads, head, 0, unroll=1 if shifted else 4)
 
         @pl.when(bound <= SAFE * SAFE)
         def _():
@@ -128,7 +128,7 @@
     )(points, w_qkv)
 
 
-def tail(points_ref, att_ref, ids_ref, wout_ref, wup_ref, wdown_ref, fin_s, means_ref):
+def tail(points_ref, att_ref, ids_ref, wout_ref, wup_ref, wdown_ref, fin_s, means_ref, midway):
     rows_all = points_ref.shape[0]
     blk = 256
     per = PATCH // blk
@@ -144,6 +144,7 @@
         return c
 
     lax.fori_loop(0, rows_all // blk, mlp, 0, unroll=2)
+    midway()
     ids = ids_ref[...] - jnp.min(ids_ref[...], axis=1, keepdims=True)
     vb = 128
 
@@ -227,7 +228,6 @@
 
     def send_all(self, data, pack, ready, extra=None, prepare=None):
         pack(0)
-        self.pass_on(ready)
         pack(1)
         self.keep((data,))
         pl.semaphore_wait(ready, PLANES - 1)
@@ -273,7 +273,7 @@
         key_ref[:, cols] = owner * 16 + rank
         return seen + jnp.sum(mark, axis=1, keepdims=True)
 
-    lax.fori_loop(0, count // step, ranks, jnp.zeros((DEVS, 1), F32))
+    lax.fori_loop(0, count // step, ranks, jnp.zeros((DEVS, 1), F32), unroll=2)
 
 
 def tag_rows(target_ref, key_ref, acc_ref, block, ranks):
@@ -372,6 +372,7 @@
     links.greet()
     block = out_ref.shape[0]
     rank_rows(target_ref, key_s, block)
+    links.pass_on(ready)
 
     def prepare():
         rank_rows(owner_ref, key_out, voxels)
@@ -453,7 +454,10 @@
 ):
     links = Links(inner)
     links.greet()
-    tail(points_ref, att_ref, ids_ref, wout_ref, wup_ref, wdown_ref, fin_s, x_ref)
+    tail(
+        points_ref, att_ref, ids_ref, wout_ref, wup_ref, wdown_ref, fin_s, x_ref,
+        lambda: links.pass_on(ready),
+    )
     out_ref[...] = jnp.zeros_like(out_ref)
     data = (send_s, False, got_s, d_send, d_recv)
     links.send_all(data, packer(links, x_ref, key_ref, send_s, 0), ready)
@@ -500,7 +504,7 @@
         out_ref[rows, :] = gelu(normalize(mm(x_ref[rows, :], w_ref[...]))).astype(BF)
         return c
 
-    lax.fori_loop(0, x_ref.shape[0] // block, some, 0)
+    lax.fori_loop(0, x_ref.shape[0] // block, some, 0, unroll=2)
 
 
 def finish(x, w):

time: 158 us -> 156 us (0.987)
  Pallas kernels: 158 us -> 156 us
where the time goes in v5:
time: 156 us
  Pallas kernels  156 us (100%)
    pallas_call x1, Pallas kernels, attention(): pl.pallas_call(attention_kernel, out_shape=jax.ShapeDtypeStruct((rows //...  68.6 us
    pallas_call x1, Pallas kernels, spread(): pl.pallas_call(functools.partial(spread_kernel, capacity - 4, inner, voxe...  56.4 us
    pallas_call x1, Pallas kernels, gather(): pl.pallas_call(functools.partial(gather_kernel, inner), out_shape=jax.Sha...  27.8 us

profile of v5, /device:TPU:1, one launch (start us, length us, event | category | flops | bytes accessed | tf_op | source)
XLA Modules:
  0.0 155.6 jit_solution(3073050424468393289)
XLA Ops:
  0.0 56.4 %spread.1 = (bf16[2048,256]{1,0:T(8,128)(2,1)}, s32[1,512]{1,0:T(1,128)}, s32[8,1,256]{2,1,0:T(1,128)}) custom-call(bf16[2048,256]{1,0:T(8,128)(2,1)} %x_ref.1, s32[1,2048]{1,0:T(1,128)} %bitcast.3, s32[1,512]{1,0:T(1,128)} %bitcast.5), custom_call_target="tpu_custom_call" | custom-call | tf_op jit(solution)/shard_map/spread/pallas_call | solution.py:430
  56.4 68.6 %attention.1.att_ref = bf16[2,256,1024]{2,1,0:T(8,128)(2,1)} custom-call(bf16[2048,256]{1,0:T(8,128)(2,1)} %get-tuple-element.8.points_ref, bf16[3,256,256]{2,1,0:T(8,128)(2,1)} %wqkv_ref.1), custom_call_target="tpu_custom_call" | custom-call | tf_op jit(solution)/shard_map/attention/pallas_call | solution.py:114
  125.1 27.8 %gather.1.x_ref = bf16[512,256]{1,0:T(8,128)(2,1)} custom-call(bf16[2048,256]{1,0:T(8,128)(2,1)} %get-tuple-element.8.points_ref, bf16[2,256,1024]{2,1,0:T(8,128)(2,1)} %attention.1.att_ref, s32[1,2048]{1,0:T(1,128)} %bitcast.4, bf16[256,256]{1,0:T(8,128)(2,1)} %wout_ref.1, bf16[256,1024]{1,0:T(8,128)(2,1)} %wup_ref.1, bf16[1024,256]{1,0:T(8,128)(2,1)} %wdown_ref.1, ...), custom_call_target="tpu_custom_call" | custom-call | tf_op jit(solution)/shard_map/gather/pallas_call | solution.py:484
  152.9 2.8 %finish.1 = bf16[512,512]{1,0:T(8,128)(2,1)} custom-call(bf16[512,256]{1,0:T(8,128)(2,1)} %gather.1.x_ref, bf16[256,512]{1,0:T(8,128)(2,1)} %w_ref.1), custom_call_target="tpu_custom_call" | custom-call | tf_op jit(solution)/shard_map/finish/pallas_call | solution.py:512

commit v6 on v5

--- a/solution.py
+++ b/solution.py
@@ -70,7 +70,7 @@
         qmax, kmax = lax.fori_loop(
             0, PATCH // blk, project,
             (jnp.zeros((heads, blk), F32), jnp.zeros((1, 128), F32)),
-            unroll=2,
+            unroll=4,
         )
         bound = 1.05 * SCALE * SCALE * jnp.max(qmax) * jnp.max(kmax)
         qb = 512
@@ -92,7 +92,7 @@
                     att_ref[number, pl.ds(r0, HS), q0 : q0 + qb] = (out[:HS] / out[HS : HS + 1]).astype(BF)
                 return c
 
-            lax.fori_loop(0, heads, head, 0, unroll=1 if shifted else 4)
+            lax.fori_loop(0, heads, head, 0, unroll=1 if shifted else 8)
 
         @pl.when(bound <= SAFE * SAFE)
         def _():
@@ -143,7 +143,7 @@
         fin_s[rows, :] = (middle + mm(hidden, wdown_ref[...])).astype(BF)
         return c
 
-    lax.fori_loop(0, rows_all // blk, mlp, 0, unroll=2)
+    lax.fori_loop(0, rows_all // blk, mlp, 0, unroll=4)
     midway()
     ids = ids_ref[...] - jnp.min(ids_ref[...], axis=1, keepdims=True)
     vb = 128
@@ -155,7 +155,7 @@
         means_ref[pl.ds(v0, vb), :] = (mm(marks.astype(BF), fin_s[...]) / tally).astype(BF)
         return c
 
-    lax.fori_loop(0, means_ref.shape[0] // vb, pool, 0, unroll=2)
+    lax.fori_loop(0, means_ref.shape[0] // vb, pool, 0, unroll=4)
 
 
 PLANES = 8
@@ -504,7 +504,7 @@
         out_ref[rows, :] = gelu(normalize(mm(x_ref[rows, :], w_ref[...]))).astype(BF)
         return c
 
-    lax.fori_loop(0, x_ref.shape[0] // block, some, 0, unroll=2)
+    lax.fori_loop(0, x_ref.shape[0] // block, some, 0, unroll=4)
 
 
 def finish(x, w):

time: 156 us -> 154 us (0.987)
  Pallas kernels: 156 us -> 154 us
where the time goes in v6:
time: 154 us
  Pallas kernels  154 us (100%)
    pallas_call x1, Pallas kernels, attention(): pl.pallas_call(attention_kernel, out_shape=jax.ShapeDtypeStruct((rows //...  68.1 us
    pallas_call x1, Pallas kernels, spread(): pl.pallas_call(functools.partial(spread_kernel, capacity - 4, inner, voxe...  56.4 us
    pallas_call x1, Pallas kernels, gather(): pl.pallas_call(functools.partial(gather_kernel, inner), out_shape=jax.Sha...  26.8 us

profile of v6, /device:TPU:1, one launch (start us, length us, event | category | flops | bytes accessed | tf_op | source)
XLA Modules:
  0.0 153.7 jit_solution(14633042786964192815)
XLA Ops:
  0.0 56.4 %spread.1 = (bf16[2048,256]{1,0:T(8,128)(2,1)}, s32[1,512]{1,0:T(1,128)}, s32[8,1,256]{2,1,0:T(1,128)}) custom-call(bf16[2048,256]{1,0:T(8,128)(2,1)} %x_ref.1, s32[1,2048]{1,0:T(1,128)} %bitcast.3, s32[1,512]{1,0:T(1,128)} %bitcast.5), custom_call_target="tpu_custom_call" | custom-call | tf_op jit(solution)/shard_map/spread/pallas_call | solution.py:430
  56.4 68.1 %attention.1.att_ref = bf16[2,256,1024]{2,1,0:T(8,128)(2,1)} custom-call(bf16[2048,256]{1,0:T(8,128)(2,1)} %get-tuple-element.8.points_ref, bf16[3,256,256]{2,1,0:T(8,128)(2,1)} %wqkv_ref.1), custom_call_target="tpu_custom_call" | custom-call | tf_op jit(solution)/shard_map/attention/pallas_call | solution.py:114
  124.5 26.8 %gather.1.x_ref = bf16[512,256]{1,0:T(8,128)(2,1)} custom-call(bf16[2048,256]{1,0:T(8,128)(2,1)} %get-tuple-element.8.points_ref, bf16[2,256,1024]{2,1,0:T(8,128)(2,1)} %attention.1.att_ref, s32[1,2048]{1,0:T(1,128)} %bitcast.4, bf16[256,256]{1,0:T(8,128)(2,1)} %wout_ref.1, bf16[256,1024]{1,0:T(8,128)(2,1)} %wup_ref.1, bf16[1024,256]{1,0:T(8,128)(2,1)} %wdown_ref.1, ...), custom_call_target="tpu_custom_call" | custom-call | tf_op jit(solution)/shard_map/gather/pallas_call | solution.py:484
  151.3 2.5 %finish.1 = bf16[512,512]{1,0:T(8,128)(2,1)} custom-call(bf16[512,256]{1,0:T(8,128)(2,1)} %gather.1.x_ref, bf16[256,512]{1,0:T(8,128)(2,1)} %w_ref.1), custom_call_target="tpu_custom_call" | custom-call | tf_op jit(solution)/shard_map/finish/pallas_call | solution.py:512
